TPU v7x, 128 devices: a whole 4x4x4 slice. The times are simulated.
128 devices in a mesh: pts: 8 (over y, core), cen: 16 (over x, z).
Axes of the slice: x: 4, y: 4, z: 4, core: 2. Of those that a mesh axis runs over, the one named last changes fastest.
Arguments:
- points: bfloat16 [32768, 1024], P('pts'), may hold values from -128 to 128
- centroids: float32 [8192, 1024], P('cen'), may hold values from -10 to 10
Outputs:
- centroid_means: float32 [8192, 1024], P('cen', 'pts')
- log_norms: float32 [32768], P('pts')
All inputs are finite; a program needn't handle non-finite values.
Results may differ from a plain program's by a relative error of at most 0.0015.
The roundings to bfloat16 on the way count: a program that leaves them out, or rounds other values in their place, can miss the bound.
Values may be sent and summed in bfloat16 or wider, within the bound.
A program may use at most 64 MiB of HBM per device.

v0:
```python
import jax
import jax.numpy as jnp
from jax import lax
from jax.sharding import PartitionSpec as P

ITERS = 2


def normalize_rows(rows, square_sums):
    return rows * lax.rsqrt(square_sums + 1e-06)[:, None]


def on_device(points, centroids):
    unit_rows = normalize_rows(centroids, jnp.sum(centroids * centroids, axis=1)).astype(
        jnp.bfloat16
    )
    ones_row = jnp.ones((1, points.shape[0]), jnp.bfloat16)
    centroid_means = centroids
    log_norms = jnp.zeros((points.shape[0],), jnp.float32)
    for iteration in range(ITERS):
        final_step = iteration + 1 == ITERS
        logits = lax.dot_general(
            points, unit_rows, (((1,), (1,)), ((), ())), preferred_element_type=jnp.float32
        )
        local_max = jnp.max(logits, axis=1)
        row_max = lax.pmax(local_max, "cen")
        shifted = jnp.exp(logits - row_max[:, None])
        row_total = lax.psum(jnp.sum(shifted, axis=1), "cen")
        weights = (shifted / row_total[:, None]).astype(jnp.bfloat16)
        log_norms = row_max + jnp.log(row_total)
        weighted = lax.dot_general(
            weights, points, (((0,), (0,)), ((), ())), preferred_element_type=jnp.float32
        )
        point_mass = jnp.dot(ones_row, weights, preferred_element_type=jnp.float32)[0]
        weighted, point_mass = lax.psum((weighted, point_mass), "pts")
        full_means = weighted / jnp.maximum(point_mass, 1.0)[:, None]
        if final_step:
            column_count = full_means.shape[1] // lax.axis_size("pts")
            centroid_means = lax.dynamic_slice_in_dim(
                full_means, lax.axis_index("pts") * column_count, column_count, 1
            )
        else:
            unit_rows = normalize_rows(full_means, jnp.sum(full_means * full_means, axis=1)).astype(
                jnp.bfloat16
            )
    return (centroid_means, log_norms)


def solution(mesh):
    placed = (P("pts", None), P("cen", None))
    return jax.shard_map(
        on_device,
        mesh=mesh,
        in_specs=placed,
        out_specs=(P("cen", "pts"), P("pts")),
        check_vma=False,
    )
```

profile of v0, /device:TPU:1, one launch (start us, length us, event | category | flops | bytes accessed | tf_op | source)
XLA Modules:
  0.0 490.7 jit_solution(4307222227081772632)
XLA Ops:
  7.2 1.8 multiply_reduce_fusion.1
  9.0 11.8 %fusion.14 = (f32[4096]{0:T(1024)S(1)}, f32[512,4096]{1,0:T(8,128)}) fusion(bf16[4096,1024]{1,0:T(8,128)(2,1)} %param.2, f32[512,1024]{1,0:T(8,128)} %param.3, f32[512]{0:T(512)S(1)} %add_rsqrt_fusion.1), kind=kOutput, calls=%fused_computation.29 | convolution fusion | flops 4298108928 | bytes 18892800 | tf_op jit(solution)/shard_map/dot_general | solution.py:22
  20.8 62.4 %pmax.14 = f32[4096]{0:T(1024)S(1)} all-reduce(f32[4096]{0:T(1024)S(1)} %get-tuple-element.2), channel_id=1, replica_groups=mesh['pts'=8,'cen'=16] {'cen'}, use_global_device_ids=true, to_apply=%region_2.0 | all-reduce | flops 4096 | bytes 32768 | tf_op jit(solution)/shard_map/pmax | solution.py:26
  83.2 4.5 fusion
  87.7 55.8 %psum.42 = f32[4096]{0:T(1024)S(1)} all-reduce(f32[4096]{0:T(1024)S(1)} %fusion), channel_id=1, replica_groups=mesh['pts'=8,'cen'=16] {'cen'}, use_global_device_ids=true, to_apply=%region_4.0 | all-reduce | flops 4096 | bytes 32768 | tf_op jit(solution)/shard_map/psum | solution.py:28
  143.5 4.1 divide_convert_fusion.1
  147.6 1.9 copy-done.1
  149.6 8.2 %fusion.16 = f32[512,1024]{1,0:T(8,128)} fusion(bf16[512,4096]{1,0:T(8,128)(2,1)S(1)} %divide_convert_fusion.1, bf16[4096,1024]{1,0:T(8,128)(2,1)} %param.2), kind=kOutput, calls=%fused_computation.31 | convolution fusion | flops 4294967296 | bytes 14680064 | tf_op jit(solution)/shard_map/dot_general | solution.py:31
  157.8 3.4 fusion.4
  161.2 40.7 %psum.44 = f32[512]{0:T(512)S(1)} all-reduce(f32[512]{0:T(512)S(1)} %bitcast.14), channel_id=1, replica_groups=mesh['pts'=8,'cen'=16] {'pts'}, use_global_device_ids=true, to_apply=%region_6.0 | all-reduce | flops 512 | bytes 4096 | tf_op jit(solution)/shard_map/psum | solution.py:35
  201.9 44.1 %all-reduce.3.cloned.1.call-done = f32[512,1024]{1,0:T(8,128)} async-done(((f32[512,1024]{1,0:T(8,128)}), f32[512,1024]{1,0:T(8,128)}) %all-reduce.3.cloned.1.call-update) | async-done | bytes 2097168 | tf_op jit(solution)/shard_map/psum | solution.py:35
  246.0 1.9 multiply_reduce_fusion
  248.0 11.9 %fusion.15 = (f32[4096]{0:T(1024)S(1)}, f32[512,4096]{1,0:T(8,128)}) fusion(bf16[4096,1024]{1,0:T(8,128)(2,1)} %param.2, f32[512]{0:T(512)S(1)} %add_rsqrt_fusion, f32[512,1024]{1,0:T(8,128)} %all-reduce.3.cloned.1.call-done, f32[512]{0:T(512)S(1)} %broadcast_maximum_fusion.1), kind=kOutput, calls=%fused_computation.30 | convolution fusion | flops 4298633216 | bytes 18894848 | tf_op jit(solution)/shard_map/dot_general | solution.py:22
  259.8 60.3 %pmax.15 = f32[4096]{0:T(1024)S(1)} all-reduce(f32[4096]{0:T(1024)S(1)} %get-tuple-element.4), channel_id=1, replica_groups=mesh['pts'=8,'cen'=16] {'cen'}, use_global_device_ids=true, to_apply=%region_9.0 | all-reduce | flops 4096 | bytes 32768 | tf_op jit(solution)/shard_map/pmax | solution.py:26
  320.1 4.5 fusion.1
  324.6 55.6 %psum.45 = f32[4096]{0:T(1024)S(1)} all-reduce(f32[4096]{0:T(1024)S(1)} %fusion.1), channel_id=1, replica_groups=mesh['pts'=8,'cen'=16] {'cen'}, use_global_device_ids=true, to_apply=%region_11.0 | all-reduce | flops 4096 | bytes 32768 | tf_op jit(solution)/shard_map/psum | solution.py:28
  380.3 4.1 divide_convert_fusion
  384.4 1.9 copy-done
  386.3 8.2 %fusion.17 = f32[512,1024]{1,0:T(8,128)} fusion(bf16[512,4096]{1,0:T(8,128)(2,1)S(1)} %divide_convert_fusion, bf16[4096,1024]{1,0:T(8,128)(2,1)} %param.2), kind=kOutput, calls=%fused_computation.32 | convolution fusion | flops 4294967296 | bytes 14680064 | tf_op jit(solution)/shard_map/dot_general | solution.py:31
  394.6 3.4 fusion.2
  397.9 42.6 %psum.47 = f32[512]{0:T(512)S(1)} all-reduce(f32[512]{0:T(512)S(1)} %bitcast.15), channel_id=1, replica_groups=mesh['pts'=8,'cen'=16] {'pts'}, use_global_device_ids=true, to_apply=%region_13.0 | all-reduce | flops 512 | bytes 4096 | tf_op jit(solution)/shard_map/psum | solution.py:35
  440.5 0.6 log_add_fusion
  441.1 41.0 %all-reduce.5.cloned.1.call-done = f32[512,1024]{1,0:T(8,128)} async-done(((f32[512,1024]{1,0:T(8,128)}), f32[512,1024]{1,0:T(8,128)}) %all-reduce.5.cloned.1.call-update) | async-done | bytes 2097168 | tf_op jit(solution)/shard_map/psum | solution.py:35
  482.1 1.8 dynamic-slice_divide_fusion
  (10 shorter events, 0.1 us)
Async XLA Ops:
  7.2 238.9 %all-reduce.3.cloned.1.call-start = ((), (), s32[]{:S(2)}) async-start(), calls=%async_computation | async-start | bytes 4194304 | tf_op jit(solution)/shard_map/psum | solution.py:35
  147.6 1.9 copy-start.1
  157.8 324.3 %all-reduce.5.cloned.1.call-start = ((), (), s32[]{:S(2)}) async-start(), calls=%async_computation.1 | async-start | bytes 4194304 | tf_op jit(solution)/shard_map/psum | solution.py:35
  384.4 1.9 copy-start
Sparse Core Ops, SparseCore 0:
  157.9 88.0 all-reduce.2
  394.7 87.3 all-reduce.4
where the time goes:
time: 492 us; the launch traced here: 491 us
  blocking collectives  317 us (64%)
  waiting for transfers between devices  85.1 us (17%)
  matrix products  46.8 us (10%)
  other arithmetic  23.5 us (5%)
  between operations  14.1 us (3%)
    pmax x2, blocking collectives, on_device(): row_max = lax.pmax(local_max, 'cen')  123 us
    psum x2, blocking collectives, on_device(): row_total = lax.psum(jnp.sum(shifted, axis=1), 'cen')  111 us
    psum x2, waiting for transfers between devices, on_device(): weighted, point_mass = lax.psum((weighted, point_mass), 'pts')  85.1 us
    psum x2, blocking collectives, on_device(): weighted, point_mass = lax.psum((weighted, point_mass), 'pts')  83.3 us
    dot_general x2, matrix products, on_device(): lax.dot_general(points, unit_rows, (((1,), (1,)), ((), ())), preferred_el...  23.7 us
    dot_general x2, matrix products, on_device(): lax.dot_general(weights, points, (((0,), (0,)), ((), ())), preferred_elem...  16.4 us
  transfers between devices with their start and end apart: 2, of which 2 were waited for; matrix products, arithmetic and copies ran while one was open for 2% of the time, Pallas kernels for 0%

commit v1 on v0

v1 whole, which is shorter than its diff:
```python
import functools
import jax
import jax.numpy as jnp
from jax import lax
from jax.experimental import pallas as pl
from jax.experimental.pallas import tpu as pltpu
from jax.sharding import PartitionSpec as P

ITERS = 2
MESH = pl.DeviceIdType.MESH
F32 = jnp.float32
BF16 = jnp.bfloat16
CHUNK = 1024
COLS = 256


def kernel(
    pts_hbm, cen_hbm, means_out, log_out,
    pts, cen, unit, expd, wts, mass, max_loc, stat, acc, pair, sib_buf, y_buf, col_buf,
    mass_all, mass_col, sums,
    in_sem, st_send, st_recv, sib_send, sib_recv, y_send, y_recv, m_send, m_recv,
    g_send, g_recv, gs_send, gs_recv,
):
    p = lax.axis_index("pts")
    c = lax.axis_index("cen")
    y, core = p // 2, lax.rem(p, 2)
    other = 1 - core
    n_chunks = pts.shape[0] // CHUNK
    n_cols = pts.shape[1] // COLS

    def at_y(k):
        return lax.rem(y + k, 4)

    def y_peer(k):
        return (at_y(k) * 2 + core, c)

    sibling = (y * 2 + other, c)

    def load_points(i):
        rows = pl.ds(pl.multiple_of(i * CHUNK, CHUNK), CHUNK)
        return pltpu.make_async_copy(pts_hbm.at[rows], pts.at[rows], in_sem.at[i])

    load_cen = pltpu.make_async_copy(cen_hbm, cen, in_sem.at[n_chunks])
    load_cen.start()

    @pl.loop(0, n_chunks)
    def _(i):
        load_points(i).start()

    barrier = pltpu.get_barrier_semaphore()

    @pl.loop(1, 16)
    def _(i):
        pl.semaphore_signal(barrier, inc=1, device_id=(p, lax.rem(c + i, 16)), device_id_type=MESH)

    @pl.loop(1, 8)
    def _(i):
        pl.semaphore_signal(barrier, inc=1, device_id=(lax.rem(p + i, 8), c), device_id_type=MESH)

    load_cen.wait()

    @pl.loop(0, 8)
    def _(b):
        rows = pl.ds(pl.multiple_of(b * 64, 64), 64)
        v = cen[rows, :]
        squares = jnp.sum(v * v, axis=1, keepdims=True)
        unit[0, rows, :] = (v * lax.rsqrt(squares + 1e-06)).astype(BF16)

    pl.semaphore_wait(barrier, 22)

    def stat_copy(it, ch, i, slot):
        return pltpu.make_async_remote_copy(
            src_ref=stat.at[it, ch, c], dst_ref=stat.at[it, ch, slot],
            send_sem=st_send.at[it, ch, i], recv_sem=st_recv.at[it, ch, slot],
            device_id=(p, lax.rem(c + i, 16)), device_id_type=MESH,
        )

    def sib_copy(it, n):
        if it == 0:
            src = acc.at[it, n, pl.ds(pl.multiple_of(other * 256, 256), 256), :]
            dst = sib_buf.at[n]
        else:
            src = acc.at[it, n, :, pl.ds(pl.multiple_of(other * 128, 128), 128)]
            dst = col_buf.at[n]
        return pltpu.make_async_remote_copy(
            src_ref=src, dst_ref=dst, send_sem=sib_send.at[it, n], recv_sem=sib_recv.at[it, n],
            device_id=sibling, device_id_type=MESH,
        )

    def y_copy_rows(n, k):
        return pltpu.make_async_remote_copy(
            src_ref=pair.at[n, pl.ds(pl.multiple_of(at_y(k) * 64, 64), 64), :],
            dst_ref=y_buf.at[n, k - 1],
            send_sem=y_send.at[0, n, k - 1], recv_sem=y_recv.at[0, n, k - 1],
            device_id=y_peer(k), device_id_type=MESH,
        )

    def offset_of(n):
        return lax.rem(jnp.where(n == 0, 2, jnp.where(n == 1, 1, jnp.where(n == 2, 3, 0))), 4)

    def y_copy_cols(n):
        k = offset_of(n)
        return pltpu.make_async_remote_copy(
            src_ref=sums.at[n], dst_ref=sums.at[4 + n],
            send_sem=y_send.at[1, n, 0], recv_sem=y_recv.at[1, n, 0],
            device_id=y_peer(k), device_id_type=MESH,
        )

    def mass_copy(it, i, slot):
        return pltpu.make_async_remote_copy(
            src_ref=mass_all.at[it, p], dst_ref=mass_all.at[it, slot],
            send_sem=m_send.at[it, i], recv_sem=m_recv.at[it, slot],
            device_id=(lax.rem(p + i, 8), c), device_id_type=MESH,
        )

    def rows_of(yy, cc):
        return pl.ds(pl.multiple_of(cc * 256 + yy * 64, 64), 64)

    def gather_y(k):
        rows = rows_of(y, core)
        return pltpu.make_async_remote_copy(
            src_ref=unit.at[1, rows], dst_ref=unit.at[1, rows],
            send_sem=g_send.at[k - 1], recv_sem=g_recv.at[k - 1],
            device_id=y_peer(k), device_id_type=MESH,
        )

    def gather_sib(k):
        rows = rows_of(at_y(4 - k), core)
        return pltpu.make_async_remote_copy(
            src_ref=unit.at[1, rows], dst_ref=unit.at[1, rows],
            send_sem=gs_send.at[k], recv_sem=gs_recv.at[k],
            device_id=sibling, device_id_type=MESH,
        )

    for it in range(ITERS):
        last = it + 1 == ITERS

        @pl.loop(0, n_chunks)
        def _(ch):
            if it == 0:
                load_points(ch).wait()
            cols = pl.ds(pl.multiple_of(ch * CHUNK, CHUNK), CHUNK)
            logits = lax.dot_general(
                unit[it], pts[cols, :], (((1,), (1,)), ((), ())), preferred_element_type=F32
            )
            local_max = jnp.max(logits, axis=0, keepdims=True)
            shifted = jnp.exp(logits - local_max)
            total = jnp.sum(shifted, axis=0, keepdims=True)
            expd[:, cols] = shifted
            lse = local_max + jnp.log(total)
            for j in range(CHUNK // 128):
                max_loc[ch, j : j + 1, :] = local_max[:, j * 128 : (j + 1) * 128]
                stat[it, ch, c, j : j + 1, :] = lse[:, j * 128 : (j + 1) * 128]

            @pl.loop(1, 16)
            def _(i):
                stat_copy(it, ch, i, c).start()

        mass[...] = jnp.zeros_like(mass)

        @pl.loop(0, n_chunks)
        def _(ch):
            @pl.loop(1, 16)
            def _(i):
                stat_copy(it, ch, i, lax.rem(c + i, 16)).wait_recv()

            every = stat[it, ch]
            row_max = jnp.max(every, axis=0)
            lse = row_max + jnp.log(jnp.sum(jnp.exp(every - row_max[None]), axis=0))
            if last:
                log_out[pl.ds(pl.multiple_of(ch * 8, 8), 8), :] = lse
            scale = jnp.exp(max_loc[ch] - lse)
            for half in range(2):
                part = None
                for j in range(half * 4, half * 4 + 4):
                    cols = pl.ds(pl.multiple_of(ch * CHUNK + j * 128, 128), 128)
                    weights = (expd[:, cols] * scale[j : j + 1, :]).astype(BF16)
                    wts[:, cols] = weights
                    wide = weights.astype(F32)
                    part = wide if part is None else part + wide
                mass[...] += part

        for b in range(4):
            block = mass[b * 128 : (b + 1) * 128, :].T
            mass_all[it, p, :, b * 128 : (b + 1) * 128] = jnp.broadcast_to(
                jnp.sum(block, axis=0, keepdims=True), (8, 128)
            )

        @pl.loop(1, 8)
        def _(i):
            mass_copy(it, i, p).start()

        def finish_pair(n):
            sib_copy(it, n).wait_recv()
            if not last:
                pair[n] = acc[it, n, pl.ds(pl.multiple_of(core * 256, 256), 256), :] + sib_buf[n]
                for k in (2, 1, 3):
                    y_copy_rows(n, k).start()
            else:
                sums[n] = acc[it, n, :, pl.ds(pl.multiple_of(core * 128, 128), 128)] + col_buf[n]

                @pl.when(n < 3)
                def _():
                    y_copy_cols(n).start()

        @pl.loop(0, n_cols)
        def _(n):
            j = at_y(offset_of(n)) if last else n
            cols = pl.ds(pl.multiple_of(j * COLS, COLS), COLS)
            acc[it, n] = jnp.dot(wts[...], pts[:, cols], preferred_element_type=F32)
            sib_copy(it, n).start()

            @pl.when(n > 0)
            def _():
                finish_pair(n - 1)

        finish_pair(n_cols - 1)

        @pl.loop(1, 8)
        def _(i):
            mass_copy(it, i, lax.rem(p + i, 8)).wait_recv()

        total_mass = jnp.sum(mass_all[it], axis=0)
        for b in range(4):
            wide = jnp.broadcast_to(total_mass[0:1, b * 128 : (b + 1) * 128], (128, 128))
            mass_col[b * 128 : (b + 1) * 128, :] = jnp.maximum(wide.T, 1.0)

        if not last:
            own = rows_of(y, core)
            own_half = pl.ds(pl.multiple_of(y * 64, 64), 64)
            divisor = mass_col[own, :]
            squares = jnp.zeros((64, 128), F32)
            for n in range(n_cols):
                for k in (1, 3, 2):
                    y_copy_rows(n, k).wait_recv()
                v = pair[n, own_half, :] + y_buf[n, 0] + y_buf[n, 1] + y_buf[n, 2]
                for h in range(COLS // 128):
                    q = v[:, h * 128 : (h + 1) * 128] / divisor
                    cen[0:64, n * COLS + h * 128 : n * COLS + (h + 1) * 128] = q
                    squares = squares + q * q
            norm = lax.rsqrt(jnp.sum(squares, axis=1, keepdims=True) + 1e-06)
            unit[1, own, :] = (cen[0:64, :] * norm).astype(BF16)
            for k in (2, 1, 3):
                gather_y(k).start()
            gather_sib(0).start()
            for k in (1, 3, 2):
                gather_y(k).wait_recv()
                gather_sib(k).start()
            for k in range(4):
                gather_sib(k).wait_recv()
        else:
            result = sums[3]
            for n in (1, 2, 0):
                y_copy_cols(n).wait_recv()
                result = result + sums[4 + n]
            means_out[...] = result / mass_col[...]

    for it in range(ITERS):

        @pl.loop(0, n_chunks)
        def _(ch):
            @pl.loop(1, 16)
            def _(i):
                stat_copy(it, ch, i, c).wait_send()

        @pl.loop(1, 8)
        def _(i):
            mass_copy(it, i, p).wait_send()

        @pl.loop(0, n_cols)
        def _(n):
            sib_copy(it, n).wait_send()

    for k in (1, 2, 3):
        gather_y(k).wait_send()
        y_copy_cols(k - 1).wait_send()

        @pl.loop(0, n_cols)
        def _(n):
            y_copy_rows(n, k).wait_send()

    for k in range(4):
        gather_sib(k).wait_send()


def on_device(points, centroids):
    n_pts, depth = points.shape
    rows = centroids.shape[0]
    n_chunks, n_cols = n_pts // CHUNK, depth // COLS
    vmem, dma = pltpu.VMEM, pltpu.SemaphoreType.DMA
    means, logs = pl.pallas_call(
        kernel,
        out_shape=(
            jax.ShapeDtypeStruct((rows, 128), F32),
            jax.ShapeDtypeStruct((n_pts // 128, 128), F32),
        ),
        in_specs=[pl.BlockSpec(memory_space=pl.ANY)] * 2,
        out_specs=(pl.BlockSpec(memory_space=pltpu.VMEM),) * 2,
        scratch_shapes=[
            vmem((n_pts, depth), BF16),
            vmem((rows, depth), F32),
            vmem((2, rows, depth), BF16),
            vmem((rows, n_pts), F32),
            vmem((rows, n_pts), BF16),
            vmem((rows, 128), F32),
            vmem((n_chunks, 8, 128), F32),
            vmem((2, n_chunks, 16, 8, 128), F32),
            vmem((2, n_cols, rows, COLS), F32),
            vmem((n_cols, rows // 2, COLS), F32),
            vmem((n_cols, rows // 2, COLS), F32),
            vmem((n_cols, 3, rows // 8, COLS), F32),
            vmem((n_cols, rows, 128), F32),
            vmem((2, 8, 8, rows), F32),
            vmem((rows, 128), F32),
            vmem((7, rows, 128), F32),
            dma((n_chunks + 1,)),
            dma((2, n_chunks, 16)), dma((2, n_chunks, 16)),
            dma((2, n_cols)), dma((2, n_cols)),
            dma((2, n_cols, 3)), dma((2, n_cols, 3)),
            dma((2, 8)), dma((2, 8)),
            dma((3,)), dma((3,)),
            dma((4,)), dma((4,)),
        ],
        compiler_params=pltpu.CompilerParams(
            collective_id=0, has_side_effects=True, vmem_limit_bytes=62 * 1024 * 1024
        ),
        name="kmeans",
    )(points, centroids)
    return means, logs.reshape(n_pts)


def solution(mesh):
    return jax.shard_map(
        on_device,
        mesh=mesh,
        in_specs=(P("pts", None), P("cen", None)),
        out_specs=(P("cen", "pts"), P("pts")),
        check_vma=False,
    )
```

time: 492 us -> 84.8 us (0.17)
  blocking collectives: 317 us -> 0 us
  waiting for transfers between devices: 85.1 us -> 0 us
  Pallas kernels: 0 us -> 80.9 us
  matrix products: 46.8 us -> 0 us
  other arithmetic: 23.5 us -> 0 us
  between operations: 14.1 us -> 0.64 us
    psum x4 -> x0, blocking collectives: 195 us -> none  [the longest x2 111 us: on_device(): row_total = lax.psum(jnp.sum(shifted, axis=1), 'cen')]
    pmax x2 -> x0, blocking collectives: 123 us -> none  [on_device(): row_max = lax.pmax(local_max, 'cen')]
    psum x2 -> x0, waiting for transfers between devices: 85.1 us -> none  [on_device(): weighted, point_mass = lax.psum((weighted, point_mass), 'pts')]
    pallas_call x0 -> x1, Pallas kernels: none -> 80.9 us  [on_device(): pl.pallas_call(kernel, out_shape=(jax.ShapeDtypeStruct((rows, 128), F32),...]
    dot_general x6 -> x0, matrix products: 46.8 us -> none  [the longest x2 23.7 us: on_device(): lax.dot_general(points, unit_rows, (((1,), (1,)), ((), ())), preferred_el...]
    reduce_sum x4 -> x0, other arithmetic: 12.8 us -> none  [the longest x2 9.06 us: on_device(): row_total = lax.psum(jnp.sum(shifted, axis=1), 'cen')]
    convert_element_type x2 -> x0, other arithmetic: 8.29 us -> none  [on_device(): weights = (shifted / row_total[:, None]).astype(jnp.bfloat16)]
  transfers between devices with their start and end apart: 2 -> 0, of which waited for: 2 -> 0; matrix products, arithmetic and copies ran while one was open for 2% -> 0% of each run, Pallas kernels for 0% -> 0%
where the time goes in v1:
time: 84.8 us; the launch traced here: 84.6 us
  Pallas kernels  80.9 us (95%)
  local copies, waits for them, and re-layouts  2.99 us (4%)
    pallas_call x1, Pallas kernels, on_device(): pl.pallas_call(kernel, out_shape=(jax.ShapeDtypeStruct((rows, 128), F32),...  80.9 us
    unnamed x2, local copies, waits for them, and re-layouts  2.99 us

profile of v1, /device:TPU:1, one launch (start us, length us, event | category | flops | bytes accessed | tf_op | source)
XLA Modules:
  0.0 84.6 jit_solution(4468487777645656481)
XLA Ops:
  0.6 80.9 %kmeans.1 = (f32[512,128]{1,0:T(8,128)}, f32[32,128]{1,0:T(8,128)}) custom-call(bf16[4096,1024]{1,0:T(8,128)(2,1)} %pts_hbm.1, f32[512,1024]{1,0:T(8,128)} %cen_hbm.1), custom_call_target="tpu_custom_call" | custom-call | tf_op jit(solution)/shard_map/kmeans/pallas_call | solution.py:291
  81.6 1.7 %copy.6 = f32[512,128]{1,0:T(8,128)} copy(f32[512,128]{1,0:T(8,128)} %get-tuple-element.8) | data formatting | bytes 524288
  83.2 1.3 %copy.7 = f32[4096]{0:T(1024)} copy(f32[4096]{0:T(1024)} %bitcast.1) | data formatting | bytes 32768

commit v2 on v1

--- a/solution.py
+++ b/solution.py
@@ -14,10 +14,32 @@
 COLS = 256
 
 
+OCTAVES = 24.0
+HALF = 117.0
+STEPS = 2.0 * HALF / OCTAVES
+
+
+def encode(ratio):
+    u = jnp.maximum(jnp.log2(jnp.abs(ratio)) + OCTAVES, 0.0) * STEPS
+    upper = jnp.floor(u)
+    value = jnp.exp2(upper - HALF) * (1.0 + (u - upper))
+    return jnp.where(ratio < 0.0, -value, value).astype(BF16)
+
+
+def decode(code):
+    value = code.astype(F32)
+    size = jnp.abs(value)
+    upper = jnp.floor(jnp.log2(size) + 0.004)
+    u = upper + (HALF - 1.0) + size * jnp.exp2(-upper)
+    ratio = jnp.exp2(u * (1.0 / STEPS) - OCTAVES)
+    ratio = jnp.where(u < 0.004, 0.0, ratio)
+    return jnp.where(value < 0.0, -ratio, ratio)
+
+
 def kernel(
     pts_hbm, cen_hbm, means_out, log_out,
-    pts, cen, unit, expd, wts, mass, max_loc, stat, acc, pair, sib_buf, y_buf, col_buf,
-    mass_all, mass_col, sums,
+    pts, cen, unit, expd, wts, mass, max_loc, stat, acc, pair, sib_buf, row_code, row_got, col_buf,
+    col_code, col_got, mass_all, inverse, bounds, mass_col,
     in_sem, st_send, st_recv, sib_send, sib_recv, y_send, y_recv, m_send, m_recv,
     g_send, g_recv, gs_send, gs_recv,
 ):
@@ -34,7 +56,8 @@
     def y_peer(k):
         return (at_y(k) * 2 + core, c)
 
-    sibling = (y * 2 + other, c)
+    sib_index = y * 2 + other
+    sibling = (sib_index, c)
 
     def load_points(i):
         rows = pl.ds(pl.multiple_of(i * CHUNK, CHUNK), CHUNK)
@@ -65,8 +88,6 @@
         v = cen[rows, :]
         squares = jnp.sum(v * v, axis=1, keepdims=True)
         unit[0, rows, :] = (v * lax.rsqrt(squares + 1e-06)).astype(BF16)
-
-    pl.semaphore_wait(barrier, 22)
 
     def stat_copy(it, ch, i, slot):
         return pltpu.make_async_remote_copy(
@@ -89,8 +110,7 @@
 
     def y_copy_rows(n, k):
         return pltpu.make_async_remote_copy(
-            src_ref=pair.at[n, pl.ds(pl.multiple_of(at_y(k) * 64, 64), 64), :],
-            dst_ref=y_buf.at[n, k - 1],
+            src_ref=row_code.at[n, k - 1], dst_ref=row_got.at[n, k - 1],
             send_sem=y_send.at[0, n, k - 1], recv_sem=y_recv.at[0, n, k - 1],
             device_id=y_peer(k), device_id_type=MESH,
         )
@@ -101,7 +121,7 @@
     def y_copy_cols(n):
         k = offset_of(n)
         return pltpu.make_async_remote_copy(
-            src_ref=sums.at[n], dst_ref=sums.at[4 + n],
+            src_ref=col_code.at[n], dst_ref=col_got.at[n],
             send_sem=y_send.at[1, n, 0], recv_sem=y_recv.at[1, n, 0],
             device_id=y_peer(k), device_id_type=MESH,
         )
@@ -152,14 +172,29 @@
                 max_loc[ch, j : j + 1, :] = local_max[:, j * 128 : (j + 1) * 128]
                 stat[it, ch, c, j : j + 1, :] = lse[:, j * 128 : (j + 1) * 128]
 
+            if it == 0:
+
+                @pl.when(ch == 0)
+                def _():
+                    pl.semaphore_wait(barrier, 22)
+
             @pl.loop(1, 16)
             def _(i):
                 stat_copy(it, ch, i, c).start()
 
         mass[...] = jnp.zeros_like(mass)
 
-        @pl.loop(0, n_chunks)
-        def _(ch):
+        if it == 0:
+            def largest(i, so_far):
+                block = pts[pl.ds(pl.multiple_of(i * 128, 128), 128), :]
+                return jnp.maximum(so_far, jnp.abs(block).reshape(8, 16, pts.shape[1]).max(axis=0))
+
+            tile = lax.fori_loop(
+                0, pts.shape[0] // 128, largest, jnp.zeros((16, pts.shape[1]), BF16)
+            )
+            size_bound = jnp.max(jnp.max(tile.astype(F32), axis=0, keepdims=True), axis=1, keepdims=True)
+
+        def weigh(ch):
             @pl.loop(1, 16)
             def _(i):
                 stat_copy(it, ch, i, lax.rem(c + i, 16)).wait_recv()
@@ -180,50 +215,94 @@
                     part = wide if part is None else part + wide
                 mass[...] += part
 
+        early = (n_chunks - 1) * CHUNK
+
+        @pl.loop(0, n_chunks - 1)
+        def _(ch):
+            weigh(ch)
+
+        def columns(n):
+            j = at_y(offset_of(n)) if last else n
+            return pl.ds(pl.multiple_of(j * COLS, COLS), COLS)
+
+        @pl.loop(0, n_cols)
+        def _(n):
+            acc[it, n] = jnp.dot(
+                wts[:, 0:early], pts[0:early, columns(n)], preferred_element_type=F32
+            )
+
+        weigh(n_chunks - 1)
+
         for b in range(4):
             block = mass[b * 128 : (b + 1) * 128, :].T
-            mass_all[it, p, :, b * 128 : (b + 1) * 128] = jnp.broadcast_to(
-                jnp.sum(block, axis=0, keepdims=True), (8, 128)
-            )
+            mass_all[it, p, 0:1, b * 128 : (b + 1) * 128] = jnp.sum(block, axis=0, keepdims=True)
+        mass_all[it, p, 1:2, :] = jnp.broadcast_to(size_bound[0:1, 0:1], (1, pair.shape[1] * 2))
 
         @pl.loop(1, 8)
         def _(i):
             mass_copy(it, i, p).start()
 
+        def chip_mass(yy):
+            row = mass_all[it, yy * 2, 0:1, :] + mass_all[it, yy * 2 + 1, 0:1, :]
+            size = jnp.maximum(mass_all[it, yy * 2, 1:2, :], mass_all[it, yy * 2 + 1, 1:2, :])
+            return row, jnp.maximum(row * size, 1e-30)
+
+        def down(row, b):
+            return jnp.broadcast_to(row[:, b * 128 : (b + 1) * 128], (128, 128)).T
+
         def finish_pair(n):
             sib_copy(it, n).wait_recv()
             if not last:
-                pair[n] = acc[it, n, pl.ds(pl.multiple_of(core * 256, 256), 256), :] + sib_buf[n]
+                half = pl.multiple_of(core * 256, 256)
+                pair[n] = acc[it, n, pl.ds(half, 256), :] + sib_buf[n]
                 for k in (2, 1, 3):
+                    at = pl.multiple_of(at_y(k) * 64, 64)
+                    for h in range(COLS // 128):
+                        lanes = slice(h * 128, (h + 1) * 128)
+                        row_code[n, k - 1, :, lanes] = encode(
+                            pair[n, pl.ds(at, 64), lanes] * inverse[pl.ds(half + at, 64), :]
+                        )
                     y_copy_rows(n, k).start()
             else:
-                sums[n] = acc[it, n, :, pl.ds(pl.multiple_of(core * 128, 128), 128)] + col_buf[n]
-
-                @pl.when(n < 3)
-                def _():
-                    y_copy_cols(n).start()
-
-        @pl.loop(0, n_cols)
+                sums = acc[it, n, :, pl.ds(pl.multiple_of(core * 128, 128), 128)] + col_buf[n]
+                if isinstance(n, int):
+                    return sums
+                col_code[n] = encode(sums * inverse[...])
+                y_copy_cols(n).start()
+
+        def finish_columns(n):
+            acc[it, n] += jnp.dot(
+                wts[:, early:], pts[early:, columns(n)], preferred_element_type=F32
+            )
+            sib_copy(it, n).start()
+
+        finish_columns(0)
+        mass_copy(it, lax.rem(8 + other - core, 8), sib_index).wait_recv()
+        _, bound = chip_mass(y)
+        for b in range(4):
+            inverse[b * 128 : (b + 1) * 128, :] = down(1.0 / bound, b)
+
+        @pl.loop(1, n_cols)
         def _(n):
-            j = at_y(offset_of(n)) if last else n
-            cols = pl.ds(pl.multiple_of(j * COLS, COLS), COLS)
-            acc[it, n] = jnp.dot(wts[...], pts[:, cols], preferred_element_type=F32)
-            sib_copy(it, n).start()
-
-            @pl.when(n > 0)
-            def _():
-                finish_pair(n - 1)
-
-        finish_pair(n_cols - 1)
+            finish_columns(n)
+            finish_pair(n - 1)
+
+        own_sum = finish_pair(n_cols - 1)
 
         @pl.loop(1, 8)
         def _(i):
-            mass_copy(it, i, lax.rem(p + i, 8)).wait_recv()
-
-        total_mass = jnp.sum(mass_all[it], axis=0)
+            @pl.when(lax.rem(p + i, 8) != sib_index)
+            def _():
+                mass_copy(it, i, lax.rem(p + i, 8)).wait_recv()
+
+        total_mass, _ = chip_mass(y)
+        for k in range(1, 4):
+            row, bound = chip_mass(at_y(4 - k))
+            total_mass = total_mass + row
+            for b in range(4):
+                bounds[k - 1, b * 128 : (b + 1) * 128, :] = down(bound, b)
         for b in range(4):
-            wide = jnp.broadcast_to(total_mass[0:1, b * 128 : (b + 1) * 128], (128, 128))
-            mass_col[b * 128 : (b + 1) * 128, :] = jnp.maximum(wide.T, 1.0)
+            mass_col[b * 128 : (b + 1) * 128, :] = jnp.maximum(down(total_mass, b), 1.0)
 
         if not last:
             own = rows_of(y, core)
@@ -233,9 +312,12 @@
             for n in range(n_cols):
                 for k in (1, 3, 2):
                     y_copy_rows(n, k).wait_recv()
-                v = pair[n, own_half, :] + y_buf[n, 0] + y_buf[n, 1] + y_buf[n, 2]
                 for h in range(COLS // 128):
-                    q = v[:, h * 128 : (h + 1) * 128] / divisor
+                    lanes = slice(h * 128, (h + 1) * 128)
+                    v = pair[n, own_half, lanes]
+                    for k in range(1, 4):
+                        v = v + decode(row_got[n, k - 1, :, lanes]) * bounds[k - 1, own, :]
+                    q = v / divisor
                     cen[0:64, n * COLS + h * 128 : n * COLS + (h + 1) * 128] = q
                     squares = squares + q * q
             norm = lax.rsqrt(jnp.sum(squares, axis=1, keepdims=True) + 1e-06)
@@ -249,10 +331,10 @@
             for k in range(4):
                 gather_sib(k).wait_recv()
         else:
-            result = sums[3]
-            for n in (1, 2, 0):
+            result = own_sum
+            for n, k in ((1, 1), (2, 3), (0, 2)):
                 y_copy_cols(n).wait_recv()
-                result = result + sums[4 + n]
+                result = result + decode(col_got[n]) * bounds[k - 1]
             means_out[...] = result / mass_col[...]
 
     for it in range(ITERS):
@@ -281,6 +363,11 @@
 
     for k in range(4):
         gather_sib(k).wait_send()
+
+
+def write_out(means, logs, means_out, log_out):
+    means_out[...] = means[...]
+    log_out[...] = logs[...]
 
 
 def on_device(points, centroids):
@@ -308,11 +395,15 @@
             vmem((2, n_cols, rows, COLS), F32),
             vmem((n_cols, rows // 2, COLS), F32),
             vmem((n_cols, rows // 2, COLS), F32),
-            vmem((n_cols, 3, rows // 8, COLS), F32),
+            vmem((n_cols, 3, rows // 8, COLS), BF16),
+            vmem((n_cols, 3, rows // 8, COLS), BF16),
             vmem((n_cols, rows, 128), F32),
+            vmem((3, rows, 128), BF16),
+            vmem((3, rows, 128), BF16),
             vmem((2, 8, 8, rows), F32),
             vmem((rows, 128), F32),
-            vmem((7, rows, 128), F32),
+            vmem((3, rows, 128), F32),
+            vmem((rows, 128), F32),
             dma((n_chunks + 1,)),
             dma((2, n_chunks, 16)), dma((2, n_chunks, 16)),
             dma((2, n_cols)), dma((2, n_cols)),
@@ -326,6 +417,15 @@
         ),
         name="kmeans",
     )(points, centroids)
+    means, logs = pl.pallas_call(
+        write_out,
+        out_shape=(
+            jax.ShapeDtypeStruct(means.shape, F32), jax.ShapeDtypeStruct(logs.shape, F32),
+        ),
+        in_specs=[pl.BlockSpec(memory_space=pltpu.VMEM)] * 2,
+        out_specs=(pl.BlockSpec(memory_space=pltpu.VMEM),) * 2,
+        name="write_out",
+    )(means, logs)
     return means, logs.reshape(n_pts)
 
 

time: 84.8 us -> 76.3 us (0.90)
  Pallas kernels: 80.9 us -> 75.6 us
  local copies, waits for them, and re-layouts: 2.99 us -> 0 us
    pallas_call x1, Pallas kernels: 80.9 us -> 73.9 us  [on_device(): pl.pallas_call(kernel, out_shape=(jax.ShapeDtypeStruct((rows, 128), F32),...]
    unnamed x2 -> x0, local copies, waits for them, and re-layouts: 2.99 us -> none
    pallas_call x0 -> x1, Pallas kernels: none -> 1.68 us  [on_device(): pl.pallas_call(write_out, out_shape=(jax.ShapeDtypeStruct(means.shape, F3...]
where the time goes in v2:
time: 76.3 us; the launch traced here: 76.2 us
  Pallas kernels  75.6 us (99%)
    pallas_call x1, Pallas kernels, on_device(): pl.pallas_call(kernel, out_shape=(jax.ShapeDtypeStruct((rows, 128), F32),...  73.9 us
    pallas_call x1, Pallas kernels, on_device(): pl.pallas_call(write_out, out_shape=(jax.ShapeDtypeStruct(means.shape, F3...  1.68 us

profile of v2, /device:TPU:1, one launch (start us, length us, event | category | flops | bytes accessed | tf_op | source)
XLA Modules:
  0.0 76.2 jit_solution(12907669212549748559)
XLA Ops:
  0.6 73.9 %kmeans.1 = (f32[512,128]{1,0:T(8,128)}, f32[32,128]{1,0:T(8,128)}) custom-call(bf16[4096,1024]{1,0:T(8,128)(2,1)} %pts_hbm.1, f32[512,1024]{1,0:T(8,128)} %cen_hbm.1), custom_call_target="tpu_custom_call" | custom-call | tf_op jit(solution)/shard_map/kmeans/pallas_call | solution.py:378
  74.5 1.7 %write_out.1 = (f32[512,128]{1,0:T(8,128)}, f32[32,128]{1,0:T(8,128)}) custom-call(f32[512,128]{1,0:T(8,128)} %get-tuple-element.6.means, f32[32,128]{1,0:T(8,128)} %get-tuple-element.7.logs), custom_call_target="tpu_custom_call" | custom-call | tf_op jit(solution)/shard_map/write_out/pallas_call | solution.py:420

commit v3 on v2

--- a/solution.py
+++ b/solution.py
@@ -92,8 +92,18 @@
     def stat_copy(it, ch, i, slot):
         return pltpu.make_async_remote_copy(
             src_ref=stat.at[it, ch, c], dst_ref=stat.at[it, ch, slot],
-            send_sem=st_send.at[it, ch, i], recv_sem=st_recv.at[it, ch, slot],
+            send_sem=st_send.at[it, ch], recv_sem=st_recv.at[it, ch],
             device_id=(p, lax.rem(c + i, 16)), device_id_type=MESH,
+        )
+
+    def offset_of(n):
+        return lax.rem(jnp.where(n == 0, 2, jnp.where(n == 1, 1, jnp.where(n == 2, 3, 0))), 4)
+
+    def all_stats(it, ch):
+        some = stat.at[it, ch, pl.ds(0, 15)]
+        return pltpu.make_async_remote_copy(
+            src_ref=some, dst_ref=some, send_sem=st_send.at[it, ch], recv_sem=st_recv.at[it, ch],
+            device_id=sibling, device_id_type=MESH,
         )
 
     def sib_copy(it, n):
@@ -101,7 +111,7 @@
             src = acc.at[it, n, pl.ds(pl.multiple_of(other * 256, 256), 256), :]
             dst = sib_buf.at[n]
         else:
-            src = acc.at[it, n, :, pl.ds(pl.multiple_of(other * 128, 128), 128)]
+            src = acc.at[it, at_y(offset_of(n)), :, pl.ds(pl.multiple_of(other * 128, 128), 128)]
             dst = col_buf.at[n]
         return pltpu.make_async_remote_copy(
             src_ref=src, dst_ref=dst, send_sem=sib_send.at[it, n], recv_sem=sib_recv.at[it, n],
@@ -115,9 +125,6 @@
             device_id=y_peer(k), device_id_type=MESH,
         )
 
-    def offset_of(n):
-        return lax.rem(jnp.where(n == 0, 2, jnp.where(n == 1, 1, jnp.where(n == 2, 3, 0))), 4)
-
     def y_copy_cols(n):
         k = offset_of(n)
         return pltpu.make_async_remote_copy(
@@ -126,10 +133,17 @@
             device_id=y_peer(k), device_id_type=MESH,
         )
 
-    def mass_copy(it, i, slot):
+    def all_masses(it, some, sem):
+        some = mass_all.at[it, pl.ds(0, some)]
+        return pltpu.make_async_remote_copy(
+            src_ref=some, dst_ref=some, send_sem=m_send.at[it], recv_sem=m_recv.at[it, sem],
+            device_id=sibling, device_id_type=MESH,
+        )
+
+    def mass_copy(it, i, slot, sem):
         return pltpu.make_async_remote_copy(
             src_ref=mass_all.at[it, p], dst_ref=mass_all.at[it, slot],
-            send_sem=m_send.at[it, i], recv_sem=m_recv.at[it, slot],
+            send_sem=m_send.at[it], recv_sem=m_recv.at[it, sem],
             device_id=(lax.rem(p + i, 8), c), device_id_type=MESH,
         )
 
@@ -195,10 +209,7 @@
             size_bound = jnp.max(jnp.max(tile.astype(F32), axis=0, keepdims=True), axis=1, keepdims=True)
 
         def weigh(ch):
-            @pl.loop(1, 16)
-            def _(i):
-                stat_copy(it, ch, i, lax.rem(c + i, 16)).wait_recv()
-
+            all_stats(it, ch).wait_recv()
             every = stat[it, ch]
             row_max = jnp.max(every, axis=0)
             lse = row_max + jnp.log(jnp.sum(jnp.exp(every - row_max[None]), axis=0))
@@ -217,19 +228,27 @@
 
         early = (n_chunks - 1) * CHUNK
 
-        @pl.loop(0, n_chunks - 1)
+        def slot(n):
+            return at_y(offset_of(n)) if last else n
+
+        def columns(n):
+            return pl.ds(pl.multiple_of(slot(n) * COLS, COLS), COLS)
+
+        def product(ch):
+            cols = pl.ds(pl.multiple_of(ch * CHUNK, CHUNK), CHUNK)
+            return jnp.dot(wts[:, cols], pts[cols, :], preferred_element_type=F32)
+
+        weigh(0)
+        first = product(0)
+        for n in range(n_cols):
+            acc[it, n] = first[:, n * COLS : (n + 1) * COLS]
+
+        @pl.loop(1, n_chunks - 1)
         def _(ch):
             weigh(ch)
-
-        def columns(n):
-            j = at_y(offset_of(n)) if last else n
-            return pl.ds(pl.multiple_of(j * COLS, COLS), COLS)
-
-        @pl.loop(0, n_cols)
-        def _(n):
-            acc[it, n] = jnp.dot(
-                wts[:, 0:early], pts[0:early, columns(n)], preferred_element_type=F32
-            )
+            more = product(ch)
+            for n in range(n_cols):
+                acc[it, n] += more[:, n * COLS : (n + 1) * COLS]
 
         weigh(n_chunks - 1)
 
@@ -238,9 +257,14 @@
             mass_all[it, p, 0:1, b * 128 : (b + 1) * 128] = jnp.sum(block, axis=0, keepdims=True)
         mass_all[it, p, 1:2, :] = jnp.broadcast_to(size_bound[0:1, 0:1], (1, pair.shape[1] * 2))
 
+        to_sib = lax.rem(8 + other - core, 8)
+        mass_copy(it, to_sib, p, 0).start()
+
         @pl.loop(1, 8)
         def _(i):
-            mass_copy(it, i, p).start()
+            @pl.when(i != to_sib)
+            def _():
+                mass_copy(it, i, p, 1).start()
 
         def chip_mass(yy):
             row = mass_all[it, yy * 2, 0:1, :] + mass_all[it, yy * 2 + 1, 0:1, :]
@@ -264,20 +288,20 @@
                         )
                     y_copy_rows(n, k).start()
             else:
-                sums = acc[it, n, :, pl.ds(pl.multiple_of(core * 128, 128), 128)] + col_buf[n]
+                sums = acc[it, slot(n), :, pl.ds(pl.multiple_of(core * 128, 128), 128)] + col_buf[n]
                 if isinstance(n, int):
                     return sums
                 col_code[n] = encode(sums * inverse[...])
                 y_copy_cols(n).start()
 
         def finish_columns(n):
-            acc[it, n] += jnp.dot(
+            acc[it, slot(n)] += jnp.dot(
                 wts[:, early:], pts[early:, columns(n)], preferred_element_type=F32
             )
             sib_copy(it, n).start()
 
         finish_columns(0)
-        mass_copy(it, lax.rem(8 + other - core, 8), sib_index).wait_recv()
+        all_masses(it, 1, 0).wait_recv()
         _, bound = chip_mass(y)
         for b in range(4):
             inverse[b * 128 : (b + 1) * 128, :] = down(1.0 / bound, b)
@@ -289,11 +313,7 @@
 
         own_sum = finish_pair(n_cols - 1)
 
-        @pl.loop(1, 8)
-        def _(i):
-            @pl.when(lax.rem(p + i, 8) != sib_index)
-            def _():
-                mass_copy(it, i, lax.rem(p + i, 8)).wait_recv()
+        all_masses(it, 6, 1).wait_recv()
 
         total_mass, _ = chip_mass(y)
         for k in range(1, 4):
@@ -341,13 +361,9 @@
 
         @pl.loop(0, n_chunks)
         def _(ch):
-            @pl.loop(1, 16)
-            def _(i):
-                stat_copy(it, ch, i, c).wait_send()
-
-        @pl.loop(1, 8)
-        def _(i):
-            mass_copy(it, i, p).wait_send()
+            all_stats(it, ch).wait_send()
+
+        all_masses(it, 7, 0).wait_send()
 
         @pl.loop(0, n_cols)
         def _(n):
@@ -405,10 +421,10 @@
             vmem((3, rows, 128), F32),
             vmem((rows, 128), F32),
             dma((n_chunks + 1,)),
-            dma((2, n_chunks, 16)), dma((2, n_chunks, 16)),
+            dma((2, n_chunks)), dma((2, n_chunks)),
             dma((2, n_cols)), dma((2, n_cols)),
             dma((2, n_cols, 3)), dma((2, n_cols, 3)),
-            dma((2, 8)), dma((2, 8)),
+            dma((2,)), dma((2, 2)),
             dma((3,)), dma((3,)),
             dma((4,)), dma((4,)),
         ],

time: 76.3 us -> 68.6 us (0.90)
  Pallas kernels: 75.6 us -> 67.8 us
    pallas_call x1, Pallas kernels: 73.9 us -> 66.2 us  [on_device(): pl.pallas_call(kernel, out_shape=(jax.ShapeDtypeStruct((rows, 128), F32),...]
where the time goes in v3:
time: 68.6 us; the launch traced here: 68.5 us
  Pallas kernels  67.8 us (99%)
    pallas_call x1, Pallas kernels, on_device(): pl.pallas_call(kernel, out_shape=(jax.ShapeDtypeStruct((rows, 128), F32),...  66.2 us
    pallas_call x1, Pallas kernels, on_device(): pl.pallas_call(write_out, out_shape=(jax.ShapeDtypeStruct(means.shape, F3...  1.68 us

profile of v3, /device:TPU:1, one launch (start us, length us, event | category | flops | bytes accessed | tf_op | source)
XLA Modules:
  0.0 68.5 jit_solution(4131514715889249320)
XLA Ops:
  0.6 66.2 %kmeans.1 = (f32[512,128]{1,0:T(8,128)}, f32[32,128]{1,0:T(8,128)}) custom-call(bf16[4096,1024]{1,0:T(8,128)(2,1)} %pts_hbm.1, f32[512,1024]{1,0:T(8,128)} %cen_hbm.1), custom_call_target="tpu_custom_call" | custom-call | tf_op jit(solution)/shard_map/kmeans/pallas_call | solution.py:394
  66.8 1.7 %write_out.1 = (f32[512,128]{1,0:T(8,128)}, f32[32,128]{1,0:T(8,128)}) custom-call(f32[512,128]{1,0:T(8,128)} %get-tuple-element.6.means, f32[32,128]{1,0:T(8,128)} %get-tuple-element.7.logs), custom_call_target="tpu_custom_call" | custom-call | tf_op jit(solution)/shard_map/write_out/pallas_call | solution.py:436

commit v4 on v3

--- a/solution.py
+++ b/solution.py
@@ -7,11 +7,13 @@
 from jax.sharding import PartitionSpec as P
 
 ITERS = 2
+VMEM_LIMIT = 52 * 1024 * 1024
 MESH = pl.DeviceIdType.MESH
 F32 = jnp.float32
 BF16 = jnp.bfloat16
 CHUNK = 1024
 COLS = 256
+GROUPS = 4
 
 
 OCTAVES = 24.0
@@ -38,7 +40,7 @@
 
 def kernel(
     pts_hbm, cen_hbm, means_out, log_out,
-    pts, cen, unit, expd, wts, mass, max_loc, stat, acc, pair, sib_buf, row_code, row_got, col_buf,
+    pts, cen, unit, expd, wts, mass, max_loc, stat, acc_rows, acc, pair, sib_buf, row_code, row_got, means_own, col_buf,
     col_code, col_got, mass_all, inverse, bounds, mass_col,
     in_sem, st_send, st_recv, sib_send, sib_recv, y_send, y_recv, m_send, m_recv,
     g_send, g_recv, gs_send, gs_recv,
@@ -49,6 +51,7 @@
     other = 1 - core
     n_chunks = pts.shape[0] // CHUNK
     n_cols = pts.shape[1] // COLS
+    half_size, own_size = pair.shape[1], pair.shape[1] // 4
 
     def at_y(k):
         return lax.rem(y + k, 4)
@@ -63,8 +66,13 @@
         rows = pl.ds(pl.multiple_of(i * CHUNK, CHUNK), CHUNK)
         return pltpu.make_async_copy(pts_hbm.at[rows], pts.at[rows], in_sem.at[i])
 
-    load_cen = pltpu.make_async_copy(cen_hbm, cen, in_sem.at[n_chunks])
-    load_cen.start()
+    def load_cen(b):
+        rows = pl.ds(pl.multiple_of(b * 128, 128), 128)
+        return pltpu.make_async_copy(cen_hbm.at[rows], cen.at[rows], in_sem.at[n_chunks + b])
+
+    @pl.loop(0, 4)
+    def _(b):
+        load_cen(b).start()
 
     @pl.loop(0, n_chunks)
     def _(i):
@@ -80,11 +88,10 @@
     def _(i):
         pl.semaphore_signal(barrier, inc=1, device_id=(lax.rem(p + i, 8), c), device_id_type=MESH)
 
-    load_cen.wait()
-
-    @pl.loop(0, 8)
+    @pl.loop(0, 4)
     def _(b):
-        rows = pl.ds(pl.multiple_of(b * 64, 64), 64)
+        load_cen(b).wait()
+        rows = pl.ds(pl.multiple_of(b * 128, 128), 128)
         v = cen[rows, :]
         squares = jnp.sum(v * v, axis=1, keepdims=True)
         unit[0, rows, :] = (v * lax.rsqrt(squares + 1e-06)).astype(BF16)
@@ -106,12 +113,17 @@
             device_id=sibling, device_id_type=MESH,
         )
 
+    def half_rows(g, cc):
+        return pl.ds(pl.multiple_of(g * 2 * half_size + cc * half_size, half_size), half_size)
+
+    def own_rows(g, yy, cc):
+        return pl.ds(pl.multiple_of(g * 2 * half_size + cc * half_size + yy * own_size, own_size), own_size)
+
     def sib_copy(it, n):
         if it == 0:
-            src = acc.at[it, n, pl.ds(pl.multiple_of(other * 256, 256), 256), :]
-            dst = sib_buf.at[n]
+            src, dst = acc_rows.at[half_rows(n, other)], sib_buf.at[n]
         else:
-            src = acc.at[it, at_y(offset_of(n)), :, pl.ds(pl.multiple_of(other * 128, 128), 128)]
+            src = acc.at[at_y(offset_of(n)), :, pl.ds(pl.multiple_of(other * 128, 128), 128)]
             dst = col_buf.at[n]
         return pltpu.make_async_remote_copy(
             src_ref=src, dst_ref=dst, send_sem=sib_send.at[it, n], recv_sem=sib_recv.at[it, n],
@@ -121,7 +133,7 @@
     def y_copy_rows(n, k):
         return pltpu.make_async_remote_copy(
             src_ref=row_code.at[n, k - 1], dst_ref=row_got.at[n, k - 1],
-            send_sem=y_send.at[0, n, k - 1], recv_sem=y_recv.at[0, n, k - 1],
+            send_sem=y_send.at[0], recv_sem=y_recv.at[0, n],
             device_id=y_peer(k), device_id_type=MESH,
         )
 
@@ -129,7 +141,7 @@
         k = offset_of(n)
         return pltpu.make_async_remote_copy(
             src_ref=col_code.at[n], dst_ref=col_got.at[n],
-            send_sem=y_send.at[1, n, 0], recv_sem=y_recv.at[1, n, 0],
+            send_sem=y_send.at[1 + n], recv_sem=y_recv.at[1, n],
             device_id=y_peer(k), device_id_type=MESH,
         )
 
@@ -147,24 +159,52 @@
             device_id=(lax.rem(p + i, 8), c), device_id_type=MESH,
         )
 
-    def rows_of(yy, cc):
-        return pl.ds(pl.multiple_of(cc * 256 + yy * 64, 64), 64)
-
-    def gather_y(k):
-        rows = rows_of(y, core)
+    def all_rows(g):
+        return pltpu.make_async_remote_copy(
+            src_ref=row_code.at[g], dst_ref=row_got.at[g],
+            send_sem=y_send.at[0], recv_sem=y_recv.at[0, g],
+            device_id=sibling, device_id_type=MESH,
+        )
+
+    def all_sent(sem):
+        return pltpu.make_async_remote_copy(
+            src_ref=row_code, dst_ref=row_code, send_sem=sem, recv_sem=y_recv.at[0, 0],
+            device_id=sibling, device_id_type=MESH,
+        )
+
+    def gather_y(g, k):
+        rows = own_rows(g, y, core)
         return pltpu.make_async_remote_copy(
             src_ref=unit.at[1, rows], dst_ref=unit.at[1, rows],
-            send_sem=g_send.at[k - 1], recv_sem=g_recv.at[k - 1],
+            send_sem=g_send.at[0], recv_sem=g_recv.at[g],
             device_id=y_peer(k), device_id_type=MESH,
         )
 
-    def gather_sib(k):
-        rows = rows_of(at_y(4 - k), core)
+    def all_gather_y(g):
+        return pltpu.make_async_remote_copy(
+            src_ref=row_code.at[g], dst_ref=row_got.at[g],
+            send_sem=g_send.at[0], recv_sem=g_recv.at[g],
+            device_id=sibling, device_id_type=MESH,
+        )
+
+    def gather_sib(g):
+        rows = half_rows(g, core)
         return pltpu.make_async_remote_copy(
             src_ref=unit.at[1, rows], dst_ref=unit.at[1, rows],
-            send_sem=gs_send.at[k], recv_sem=gs_recv.at[k],
-            device_id=sibling, device_id_type=MESH,
-        )
+            send_sem=gs_send.at[g], recv_sem=gs_recv.at[g],
+            device_id=sibling, device_id_type=MESH,
+        )
+
+    def sent(it):
+        @pl.loop(0, n_chunks)
+        def _(ch):
+            all_stats(it, ch).wait_send()
+
+        all_masses(it, 7, 0).wait_send()
+
+        @pl.loop(0, n_cols)
+        def _(n):
+            sib_copy(it, n).wait_send()
 
     for it in range(ITERS):
         last = it + 1 == ITERS
@@ -192,8 +232,7 @@
                 def _():
                     pl.semaphore_wait(barrier, 22)
 
-            @pl.loop(1, 16)
-            def _(i):
+            for i in range(1, 16):
                 stat_copy(it, ch, i, c).start()
 
         mass[...] = jnp.zeros_like(mass)
@@ -217,14 +256,12 @@
                 log_out[pl.ds(pl.multiple_of(ch * 8, 8), 8), :] = lse
             scale = jnp.exp(max_loc[ch] - lse)
             for half in range(2):
-                part = None
-                for j in range(half * 4, half * 4 + 4):
-                    cols = pl.ds(pl.multiple_of(ch * CHUNK + j * 128, 128), 128)
-                    weights = (expd[:, cols] * scale[j : j + 1, :]).astype(BF16)
-                    wts[:, cols] = weights
-                    wide = weights.astype(F32)
-                    part = wide if part is None else part + wide
-                mass[...] += part
+                cols = pl.ds(pl.multiple_of(ch * CHUNK + half * 512, 512), 512)
+                row = jnp.concatenate([scale[j : j + 1, :] for j in range(half * 4, half * 4 + 4)], axis=1)
+                weights = (expd[:, cols] * row).astype(BF16)
+                wts[:, cols] = weights
+                wide = weights.astype(F32)
+                mass[...] += sum(wide[:, a : a + 128] for a in range(0, 512, 128))
 
         early = (n_chunks - 1) * CHUNK
 
@@ -240,22 +277,28 @@
 
         weigh(0)
         first = product(0)
-        for n in range(n_cols):
-            acc[it, n] = first[:, n * COLS : (n + 1) * COLS]
+        if last:
+            for n in range(n_cols):
+                acc[n] = first[:, n * COLS : (n + 1) * COLS]
+        else:
+            acc_rows[...] = first
 
         @pl.loop(1, n_chunks - 1)
         def _(ch):
             weigh(ch)
             more = product(ch)
-            for n in range(n_cols):
-                acc[it, n] += more[:, n * COLS : (n + 1) * COLS]
+            if last:
+                for n in range(n_cols):
+                    acc[n] += more[:, n * COLS : (n + 1) * COLS]
+            else:
+                acc_rows[...] += more
 
         weigh(n_chunks - 1)
 
         for b in range(4):
             block = mass[b * 128 : (b + 1) * 128, :].T
             mass_all[it, p, 0:1, b * 128 : (b + 1) * 128] = jnp.sum(block, axis=0, keepdims=True)
-        mass_all[it, p, 1:2, :] = jnp.broadcast_to(size_bound[0:1, 0:1], (1, pair.shape[1] * 2))
+        mass_all[it, p, 1:2, :] = jnp.broadcast_to(size_bound[0:1, 0:1], (1, mass_all.shape[3]))
 
         to_sib = lax.rem(8 + other - core, 8)
         mass_copy(it, to_sib, p, 0).start()
@@ -277,30 +320,32 @@
         def finish_pair(n):
             sib_copy(it, n).wait_recv()
             if not last:
-                half = pl.multiple_of(core * 256, 256)
-                pair[n] = acc[it, n, pl.ds(half, 256), :] + sib_buf[n]
+                pair[n] = acc_rows[half_rows(n, core), :] + sib_buf[n]
                 for k in (2, 1, 3):
-                    at = pl.multiple_of(at_y(k) * 64, 64)
-                    for h in range(COLS // 128):
+                    at = pl.multiple_of(at_y(k) * own_size, own_size)
+                    scale = inverse[own_rows(n, at_y(k), core), :]
+                    for h in range(pts.shape[1] // 128):
                         lanes = slice(h * 128, (h + 1) * 128)
-                        row_code[n, k - 1, :, lanes] = encode(
-                            pair[n, pl.ds(at, 64), lanes] * inverse[pl.ds(half + at, 64), :]
-                        )
+                        row_code[n, k - 1, :, lanes] = encode(pair[n, pl.ds(at, own_size), lanes] * scale)
                     y_copy_rows(n, k).start()
             else:
-                sums = acc[it, slot(n), :, pl.ds(pl.multiple_of(core * 128, 128), 128)] + col_buf[n]
+                sums = acc[slot(n), :, pl.ds(pl.multiple_of(core * 128, 128), 128)] + col_buf[n]
                 if isinstance(n, int):
                     return sums
                 col_code[n] = encode(sums * inverse[...])
                 y_copy_cols(n).start()
 
-        def finish_columns(n):
-            acc[it, slot(n)] += jnp.dot(
-                wts[:, early:], pts[early:, columns(n)], preferred_element_type=F32
-            )
+        def finish_sums(n):
+            if last:
+                acc[slot(n)] += jnp.dot(
+                    wts[:, early:], pts[early:, columns(n)], preferred_element_type=F32
+                )
+            else:
+                rows = pl.ds(pl.multiple_of(n * 2 * half_size, half_size), 2 * half_size)
+                acc_rows[rows, :] += jnp.dot(wts[rows, early:], pts[early:, :], preferred_element_type=F32)
             sib_copy(it, n).start()
 
-        finish_columns(0)
+        finish_sums(0)
         all_masses(it, 1, 0).wait_recv()
         _, bound = chip_mass(y)
         for b in range(4):
@@ -308,7 +353,7 @@
 
         @pl.loop(1, n_cols)
         def _(n):
-            finish_columns(n)
+            finish_sums(n)
             finish_pair(n - 1)
 
         own_sum = finish_pair(n_cols - 1)
@@ -325,60 +370,53 @@
             mass_col[b * 128 : (b + 1) * 128, :] = jnp.maximum(down(total_mass, b), 1.0)
 
         if not last:
-            own = rows_of(y, core)
-            own_half = pl.ds(pl.multiple_of(y * 64, 64), 64)
-            divisor = mass_col[own, :]
-            squares = jnp.zeros((64, 128), F32)
-            for n in range(n_cols):
-                for k in (1, 3, 2):
-                    y_copy_rows(n, k).wait_recv()
-                for h in range(COLS // 128):
+            @pl.loop(0, GROUPS)
+            def _(g):
+                all_rows(g).wait_recv()
+                own = own_rows(g, y, core)
+                at = pl.ds(pl.multiple_of(y * own_size, own_size), own_size)
+                divisor = mass_col[own, :]
+                squares = jnp.zeros((own_size, 128), F32)
+                for h in range(pts.shape[1] // 128):
                     lanes = slice(h * 128, (h + 1) * 128)
-                    v = pair[n, own_half, lanes]
+                    v = pair[g, at, lanes]
                     for k in range(1, 4):
-                        v = v + decode(row_got[n, k - 1, :, lanes]) * bounds[k - 1, own, :]
+                        v = v + decode(row_got[g, k - 1, :, lanes]) * bounds[k - 1, own, :]
                     q = v / divisor
-                    cen[0:64, n * COLS + h * 128 : n * COLS + (h + 1) * 128] = q
+                    means_own[:, lanes] = q
                     squares = squares + q * q
-            norm = lax.rsqrt(jnp.sum(squares, axis=1, keepdims=True) + 1e-06)
-            unit[1, own, :] = (cen[0:64, :] * norm).astype(BF16)
-            for k in (2, 1, 3):
-                gather_y(k).start()
-            gather_sib(0).start()
-            for k in (1, 3, 2):
-                gather_y(k).wait_recv()
-                gather_sib(k).start()
-            for k in range(4):
-                gather_sib(k).wait_recv()
+                norm = lax.rsqrt(jnp.sum(squares, axis=1, keepdims=True) + 1e-06)
+                unit[1, own, :] = (means_own[...] * norm).astype(BF16)
+                for k in (2, 1, 3):
+                    gather_y(g, k).start()
+
+            sent(it)
+            all_sent(y_send.at[0]).wait_send()
+
+            @pl.loop(0, GROUPS)
+            def _(g):
+                all_gather_y(g).wait_recv()
+                gather_sib(g).start()
+
+            @pl.loop(0, GROUPS)
+            def _(g):
+                gather_sib(g).wait_recv()
         else:
+            sent(it)
+            all_sent(g_send.at[0]).wait_send()
+
+            @pl.loop(0, GROUPS)
+            def _(g):
+                gather_sib(g).wait_send()
+
             result = own_sum
-            for n, k in ((1, 1), (2, 3), (0, 2)):
+            for n, k in ((0, 2), (1, 1), (2, 3)):
                 y_copy_cols(n).wait_recv()
                 result = result + decode(col_got[n]) * bounds[k - 1]
             means_out[...] = result / mass_col[...]
 
-    for it in range(ITERS):
-
-        @pl.loop(0, n_chunks)
-        def _(ch):
-            all_stats(it, ch).wait_send()
-
-        all_masses(it, 7, 0).wait_send()
-
-        @pl.loop(0, n_cols)
-        def _(n):
-            sib_copy(it, n).wait_send()
-
-    for k in (1, 2, 3):
-        gather_y(k).wait_send()
-        y_copy_cols(k - 1).wait_send()
-
-        @pl.loop(0, n_cols)
-        def _(n):
-            y_copy_rows(n, k).wait_send()
-
-    for k in range(4):
-        gather_sib(k).wait_send()
+    for n in range(3):
+        y_copy_cols(n).wait_send()
 
 
 def write_out(means, logs, means_out, log_out):
@@ -390,6 +428,7 @@
     n_pts, depth = points.shape
     rows = centroids.shape[0]
     n_chunks, n_cols = n_pts // CHUNK, depth // COLS
+    half, own = rows // (2 * GROUPS), rows // (8 * GROUPS)
     vmem, dma = pltpu.VMEM, pltpu.SemaphoreType.DMA
     means, logs = pl.pallas_call(
         kernel,
@@ -397,7 +436,7 @@
             jax.ShapeDtypeStruct((rows, 128), F32),
             jax.ShapeDtypeStruct((n_pts // 128, 128), F32),
         ),
-        in_specs=[pl.BlockSpec(memory_space=pl.ANY)] * 2,
+        in_specs=[pl.BlockSpec(memory_space=pltpu.HBM)] * 2,
         out_specs=(pl.BlockSpec(memory_space=pltpu.VMEM),) * 2,
         scratch_shapes=[
             vmem((n_pts, depth), BF16),
@@ -408,11 +447,13 @@
             vmem((rows, 128), F32),
             vmem((n_chunks, 8, 128), F32),
             vmem((2, n_chunks, 16, 8, 128), F32),
-            vmem((2, n_cols, rows, COLS), F32),
-            vmem((n_cols, rows // 2, COLS), F32),
-            vmem((n_cols, rows // 2, COLS), F32),
-            vmem((n_cols, 3, rows // 8, COLS), BF16),
-            vmem((n_cols, 3, rows // 8, COLS), BF16),
+            vmem((rows, depth), F32),
+            vmem((n_cols, rows, COLS), F32),
+            vmem((GROUPS, half, depth), F32),
+            vmem((GROUPS, half, depth), F32),
+            vmem((GROUPS, 3, own, depth), BF16),
+            vmem((GROUPS, 3, own, depth), BF16),
+            vmem((own, depth), F32),
             vmem((n_cols, rows, 128), F32),
             vmem((3, rows, 128), BF16),
             vmem((3, rows, 128), BF16),
@@ -420,16 +461,16 @@
             vmem((rows, 128), F32),
             vmem((3, rows, 128), F32),
             vmem((rows, 128), F32),
-            dma((n_chunks + 1,)),
+            dma((n_chunks + 4,)),
             dma((2, n_chunks)), dma((2, n_chunks)),
             dma((2, n_cols)), dma((2, n_cols)),
-            dma((2, n_cols, 3)), dma((2, n_cols, 3)),
+            dma((4,)), dma((2, 4)),
             dma((2,)), dma((2, 2)),
-            dma((3,)), dma((3,)),
-            dma((4,)), dma((4,)),
+            dma((1,)), dma((GROUPS,)),
+            dma((GROUPS,)), dma((GROUPS,)),
         ],
         compiler_params=pltpu.CompilerParams(
-            collective_id=0, has_side_effects=True, vmem_limit_bytes=62 * 1024 * 1024
+            collective_id=0, has_side_effects=True, vmem_limit_bytes=VMEM_LIMIT
         ),
         name="kmeans",
     )(points, centroids)
@@ -440,6 +481,7 @@
         ),
         in_specs=[pl.BlockSpec(memory_space=pltpu.VMEM)] * 2,
         out_specs=(pl.BlockSpec(memory_space=pltpu.VMEM),) * 2,
+        compiler_params=pltpu.CompilerParams(vmem_limit_bytes=4 * 1024 * 1024),
         name="write_out",
     )(means, logs)
     return means, logs.reshape(n_pts)

time: 68.6 us -> 62.9 us (0.917)
  Pallas kernels: 67.8 us -> 62.1 us
    pallas_call x1, Pallas kernels: 66.2 us -> 61.4 us  [on_device(): pl.pallas_call(kernel, out_shape=(jax.ShapeDtypeStruct((rows, 128), F32),...]
    pallas_call x1, Pallas kernels: 1.68 us -> 0.72 us  [on_device(): pl.pallas_call(write_out, out_shape=(jax.ShapeDtypeStruct(means.shape, F3...]
where the time goes in v4:
time: 62.9 us; the launch traced here: 62.8 us
  Pallas kernels  62.1 us (99%)
  between operations  0.64 us (1%)
    pallas_call x1, Pallas kernels, on_device(): pl.pallas_call(kernel, out_shape=(jax.ShapeDtypeStruct((rows, 128), F32),...  61.4 us

profile of v4, /device:TPU:1, one launch (start us, length us, event | category | flops | bytes accessed | tf_op | source)
XLA Modules:
  0.0 62.8 jit_solution(3784715674071229471)
XLA Ops:
  0.6 61.4 %kmeans.1 = (f32[512,128]{1,0:T(8,128)S(1)}, f32[32,128]{1,0:T(8,128)S(1)}) custom-call(bf16[4096,1024]{1,0:T(8,128)(2,1)} %pts_hbm.1, f32[512,1024]{1,0:T(8,128)} %cen_hbm.1), custom_call_target="tpu_custom_call" | custom-call | tf_op jit(solution)/shard_map/kmeans/pallas_call | solution.py:433
  62.1 0.7 %write_out.1 = (f32[512,128]{1,0:T(8,128)}, f32[32,128]{1,0:T(8,128)}) custom-call(f32[512,128]{1,0:T(8,128)S(1)} %get-tuple-element.6.means, f32[32,128]{1,0:T(8,128)S(1)} %get-tuple-element.7.logs), custom_call_target="tpu_custom_call" | custom-call | tf_op jit(solution)/shard_map/write_out/pallas_call | solution.py:477

commit v5 on v4

--- a/solution.py
+++ b/solution.py
@@ -13,6 +13,10 @@
 BF16 = jnp.bfloat16
 CHUNK = 1024
 COLS = 256
+FAR_FIRST = sorted(
+    ((dx, dz) for dx in range(4) for dz in range(4) if dx or dz),
+    key=lambda d: -min(d[0], 4 - d[0]) - min(d[1], 4 - d[1]),
+)
 GROUPS = 4
 
 
@@ -53,6 +57,9 @@
     n_cols = pts.shape[1] // COLS
     half_size, own_size = pair.shape[1], pair.shape[1] // 4
 
+    def cen_peer(dx, dz):
+        return lax.rem(c // 4 + dx, 4) * 4 + lax.rem(lax.rem(c, 4) + dz, 4)
+
     def at_y(k):
         return lax.rem(y + k, 4)
 
@@ -80,13 +87,12 @@
 
     barrier = pltpu.get_barrier_semaphore()
 
-    @pl.loop(1, 16)
-    def _(i):
-        pl.semaphore_signal(barrier, inc=1, device_id=(p, lax.rem(c + i, 16)), device_id_type=MESH)
-
-    @pl.loop(1, 8)
-    def _(i):
-        pl.semaphore_signal(barrier, inc=1, device_id=(lax.rem(p + i, 8), c), device_id_type=MESH)
+    for dx, dz in FAR_FIRST:
+        pl.semaphore_signal(barrier, inc=1, device_id=(p, cen_peer(dx, dz)), device_id_type=MESH)
+    pl.semaphore_signal(barrier, inc=1, device_id=sibling, device_id_type=MESH)
+    for k in (2, 1, 3):
+        for cc in (core, other):
+            pl.semaphore_signal(barrier, inc=1, device_id=(at_y(k) * 2 + cc, c), device_id_type=MESH)
 
     @pl.loop(0, 4)
     def _(b):
@@ -96,11 +102,11 @@
         squares = jnp.sum(v * v, axis=1, keepdims=True)
         unit[0, rows, :] = (v * lax.rsqrt(squares + 1e-06)).astype(BF16)
 
-    def stat_copy(it, ch, i, slot):
-        return pltpu.make_async_remote_copy(
-            src_ref=stat.at[it, ch, c], dst_ref=stat.at[it, ch, slot],
+    def stat_copy(it, ch, peer):
+        return pltpu.make_async_remote_copy(
+            src_ref=stat.at[it, ch, c], dst_ref=stat.at[it, ch, c],
             send_sem=st_send.at[it, ch], recv_sem=st_recv.at[it, ch],
-            device_id=(p, lax.rem(c + i, 16)), device_id_type=MESH,
+            device_id=(p, peer), device_id_type=MESH,
         )
 
     def offset_of(n):
@@ -152,11 +158,11 @@
             device_id=sibling, device_id_type=MESH,
         )
 
-    def mass_copy(it, i, slot, sem):
-        return pltpu.make_async_remote_copy(
-            src_ref=mass_all.at[it, p], dst_ref=mass_all.at[it, slot],
+    def mass_copy(it, peer, sem):
+        return pltpu.make_async_remote_copy(
+            src_ref=mass_all.at[it, p], dst_ref=mass_all.at[it, p],
             send_sem=m_send.at[it], recv_sem=m_recv.at[it, sem],
-            device_id=(lax.rem(p + i, 8), c), device_id_type=MESH,
+            device_id=(peer, c), device_id_type=MESH,
         )
 
     def all_rows(g):
@@ -232,8 +238,8 @@
                 def _():
                     pl.semaphore_wait(barrier, 22)
 
-            for i in range(1, 16):
-                stat_copy(it, ch, i, c).start()
+            for dx, dz in FAR_FIRST:
+                stat_copy(it, ch, cen_peer(dx, dz)).start()
 
         mass[...] = jnp.zeros_like(mass)
 
@@ -295,19 +301,27 @@
 
         weigh(n_chunks - 1)
 
+        def finish_sums(n):
+            if last:
+                acc[slot(n)] += jnp.dot(
+                    wts[:, early:], pts[early:, columns(n)], preferred_element_type=F32
+                )
+            else:
+                rows = pl.ds(pl.multiple_of(n * 2 * half_size, half_size), 2 * half_size)
+                acc_rows[rows, :] += jnp.dot(wts[rows, early:], pts[early:, :], preferred_element_type=F32)
+            sib_copy(it, n).start()
+
         for b in range(4):
             block = mass[b * 128 : (b + 1) * 128, :].T
             mass_all[it, p, 0:1, b * 128 : (b + 1) * 128] = jnp.sum(block, axis=0, keepdims=True)
         mass_all[it, p, 1:2, :] = jnp.broadcast_to(size_bound[0:1, 0:1], (1, mass_all.shape[3]))
 
-        to_sib = lax.rem(8 + other - core, 8)
-        mass_copy(it, to_sib, p, 0).start()
-
-        @pl.loop(1, 8)
-        def _(i):
-            @pl.when(i != to_sib)
-            def _():
-                mass_copy(it, i, p, 1).start()
+        mass_copy(it, sib_index, 0).start()
+        for k in (2, 1, 3):
+            for cc in (core, other):
+                mass_copy(it, at_y(k) * 2 + cc, 1).start()
+
+        finish_sums(0)
 
         def chip_mass(yy):
             row = mass_all[it, yy * 2, 0:1, :] + mass_all[it, yy * 2 + 1, 0:1, :]
@@ -335,17 +349,6 @@
                 col_code[n] = encode(sums * inverse[...])
                 y_copy_cols(n).start()
 
-        def finish_sums(n):
-            if last:
-                acc[slot(n)] += jnp.dot(
-                    wts[:, early:], pts[early:, columns(n)], preferred_element_type=F32
-                )
-            else:
-                rows = pl.ds(pl.multiple_of(n * 2 * half_size, half_size), 2 * half_size)
-                acc_rows[rows, :] += jnp.dot(wts[rows, early:], pts[early:, :], preferred_element_type=F32)
-            sib_copy(it, n).start()
-
-        finish_sums(0)
         all_masses(it, 1, 0).wait_recv()
         _, bound = chip_mass(y)
         for b in range(4):

time: 62.9 us -> 62.6 us (level)
  no operation moved by 1% of the time
where the time goes in v5:
time: 62.6 us; the launch traced here: 62.4 us
  Pallas kernels  61.8 us (99%)
  between operations  0.64 us (1%)
    pallas_call x1, Pallas kernels, on_device(): pl.pallas_call(kernel, out_shape=(jax.ShapeDtypeStruct((rows, 128), F32),...  61.1 us

profile of v5, /device:TPU:1, one launch (start us, length us, event | category | flops | bytes accessed | tf_op | source)
XLA Modules:
  0.0 62.4 jit_solution(6811130747519140455)
XLA Ops:
  0.6 61.1 %kmeans.1 = (f32[512,128]{1,0:T(8,128)S(1)}, f32[32,128]{1,0:T(8,128)S(1)}) custom-call(bf16[4096,1024]{1,0:T(8,128)(2,1)} %pts_hbm.1, f32[512,1024]{1,0:T(8,128)} %cen_hbm.1), custom_call_target="tpu_custom_call" | custom-call | tf_op jit(solution)/shard_map/kmeans/pallas_call | solution.py:436
  61.7 0.7 %write_out.1 = (f32[512,128]{1,0:T(8,128)}, f32[32,128]{1,0:T(8,128)}) custom-call(f32[512,128]{1,0:T(8,128)S(1)} %get-tuple-element.6.means, f32[32,128]{1,0:T(8,128)S(1)} %get-tuple-element.7.logs), custom_call_target="tpu_custom_call" | custom-call | tf_op jit(solution)/shard_map/write_out/pallas_call | solution.py:480

commit v6 on v5

--- a/solution.py
+++ b/solution.py
@@ -45,7 +45,7 @@
 def kernel(
     pts_hbm, cen_hbm, means_out, log_out,
     pts, cen, unit, expd, wts, mass, max_loc, stat, acc_rows, acc, pair, sib_buf, row_code, row_got, means_own, col_buf,
-    col_code, col_got, mass_all, inverse, bounds, mass_col,
+    col_code, col_got, mass_all, inverse, bounds, mass_col, largest,
     in_sem, st_send, st_recv, sib_send, sib_recv, y_send, y_recv, m_send, m_recv,
     g_send, g_recv, gs_send, gs_recv,
 ):
@@ -85,6 +85,7 @@
     def _(i):
         load_points(i).start()
 
+    largest[...] = jnp.zeros_like(largest)
     barrier = pltpu.get_barrier_semaphore()
 
     for dx, dz in FAR_FIRST:
@@ -223,6 +224,9 @@
             logits = lax.dot_general(
                 unit[it], pts[cols, :], (((1,), (1,)), ((), ())), preferred_element_type=F32
             )
+            if it == 0:
+                tiles = jnp.abs(pts[cols, :]).reshape(CHUNK // 16, 16, pts.shape[1])
+                largest[...] = jnp.maximum(largest[...], jnp.max(tiles, axis=0))
             local_max = jnp.max(logits, axis=0, keepdims=True)
             shifted = jnp.exp(logits - local_max)
             total = jnp.sum(shifted, axis=0, keepdims=True)
@@ -244,14 +248,7 @@
         mass[...] = jnp.zeros_like(mass)
 
         if it == 0:
-            def largest(i, so_far):
-                block = pts[pl.ds(pl.multiple_of(i * 128, 128), 128), :]
-                return jnp.maximum(so_far, jnp.abs(block).reshape(8, 16, pts.shape[1]).max(axis=0))
-
-            tile = lax.fori_loop(
-                0, pts.shape[0] // 128, largest, jnp.zeros((16, pts.shape[1]), BF16)
-            )
-            size_bound = jnp.max(jnp.max(tile.astype(F32), axis=0, keepdims=True), axis=1, keepdims=True)
+            size_bound = jnp.max(jnp.max(largest[...].astype(F32), axis=0, keepdims=True), axis=1, keepdims=True)
 
         def weigh(ch):
             all_stats(it, ch).wait_recv()
@@ -464,6 +461,7 @@
             vmem((rows, 128), F32),
             vmem((3, rows, 128), F32),
             vmem((rows, 128), F32),
+            vmem((16, depth), BF16),
             dma((n_chunks + 4,)),
             dma((2, n_chunks)), dma((2, n_chunks)),
             dma((2, n_cols)), dma((2, n_cols)),

time: 62.6 us -> 62.4 us (level)
  no operation moved by 1% of the time
where the time goes in v6:
time: 62.4 us; the launch traced here: 62.3 us
  Pallas kernels  61.7 us (99%)
  between operations  0.64 us (1%)
    pallas_call x1, Pallas kernels, on_device(): pl.pallas_call(kernel, out_shape=(jax.ShapeDtypeStruct((rows, 128), F32),...  61 us

profile of v6, /device:TPU:1, one launch (start us, length us, event | category | flops | bytes accessed | tf_op | source)
XLA Modules:
  0.0 62.3 jit_solution(10458861029858151826)
XLA Ops:
  0.6 61.0 %kmeans.1 = (f32[512,128]{1,0:T(8,128)S(1)}, f32[32,128]{1,0:T(8,128)S(1)}) custom-call(bf16[4096,1024]{1,0:T(8,128)(2,1)} %pts_hbm.1, f32[512,1024]{1,0:T(8,128)} %cen_hbm.1), custom_call_target="tpu_custom_call" | custom-call | tf_op jit(solution)/shard_map/kmeans/pallas_call | solution.py:433
  61.6 0.7 %write_out.1 = (f32[512,128]{1,0:T(8,128)}, f32[32,128]{1,0:T(8,128)}) custom-call(f32[512,128]{1,0:T(8,128)S(1)} %get-tuple-element.6.means, f32[32,128]{1,0:T(8,128)S(1)} %get-tuple-element.7.logs), custom_call_target="tpu_custom_call" | custom-call | tf_op jit(solution)/shard_map/write_out/pallas_call | solution.py:478

commit v7 on v6

--- a/solution.py
+++ b/solution.py
@@ -367,7 +367,7 @@
             for b in range(4):
                 bounds[k - 1, b * 128 : (b + 1) * 128, :] = down(bound, b)
         for b in range(4):
-            mass_col[b * 128 : (b + 1) * 128, :] = jnp.maximum(down(total_mass, b), 1.0)
+            mass_col[b * 128 : (b + 1) * 128, :] = down(1.0 / jnp.maximum(total_mass, 1.0), b)
 
         if not last:
             @pl.loop(0, GROUPS)
@@ -382,7 +382,7 @@
                     v = pair[g, at, lanes]
                     for k in range(1, 4):
                         v = v + decode(row_got[g, k - 1, :, lanes]) * bounds[k - 1, own, :]
-                    q = v / divisor
+                    q = v * divisor
                     means_own[:, lanes] = q
                     squares = squares + q * q
                 norm = lax.rsqrt(jnp.sum(squares, axis=1, keepdims=True) + 1e-06)
@@ -413,7 +413,7 @@
             for n, k in ((0, 2), (1, 1), (2, 3)):
                 y_copy_cols(n).wait_recv()
                 result = result + decode(col_got[n]) * bounds[k - 1]
-            means_out[...] = result / mass_col[...]
+            means_out[...] = result * mass_col[...]
 
     for n in range(3):
         y_copy_cols(n).wait_send()

time: 62.4 us -> 62.4 us (level)
  no operation moved by 1% of the time
where the time goes in v7:
time: 62.4 us; the launch traced here: 62.3 us
  Pallas kernels  61.7 us (99%)
  between operations  0.64 us (1%)
    pallas_call x1, Pallas kernels, on_device(): pl.pallas_call(kernel, out_shape=(jax.ShapeDtypeStruct((rows, 128), F32),...  60.9 us

profile of v7, /device:TPU:1, one launch (start us, length us, event | category | flops | bytes accessed | tf_op | source)
XLA Modules:
  0.0 62.3 jit_solution(18130758073071444133)
XLA Ops:
  0.6 60.9 %kmeans.1 = (f32[512,128]{1,0:T(8,128)S(1)}, f32[32,128]{1,0:T(8,128)S(1)}) custom-call(bf16[4096,1024]{1,0:T(8,128)(2,1)} %pts_hbm.1, f32[512,1024]{1,0:T(8,128)} %cen_hbm.1), custom_call_target="tpu_custom_call" | custom-call | tf_op jit(solution)/shard_map/kmeans/pallas_call | solution.py:433
  61.6 0.7 %write_out.1 = (f32[512,128]{1,0:T(8,128)}, f32[32,128]{1,0:T(8,128)}) custom-call(f32[512,128]{1,0:T(8,128)S(1)} %get-tuple-element.6.means, f32[32,128]{1,0:T(8,128)S(1)} %get-tuple-element.7.logs), custom_call_target="tpu_custom_call" | custom-call | tf_op jit(solution)/shard_map/write_out/pallas_call | solution.py:478
